TPU v7x, 32 devices: a whole 2x2x4 slice. The times are simulated.
32 devices in a mesh: gx: 8 (over z, core), gy: 4 (over y, x).
Axes of the slice: x: 2, y: 2, z: 4, core: 2. Of those that a mesh axis runs over, the one named last changes fastest.
Arguments:
- source: float32 [128, 128, 512], P('gx', 'gy'), may hold values from -80 to 80
- conductivity: float32 [128, 128, 512], P('gx', 'gy'), may hold values from 1 to 4
Outputs:
- mid_field: float32 [128, 128, 512], P('gx', 'gy')
- new_field: float32 [128, 128, 512], P('gx', 'gy')
All inputs are finite; a program needn't handle non-finite values.
Results may differ from a plain program's by a relative error of at most 0.0003.
Values sent between devices are 32-bit elements; how exact they have to be, the bound alone decides.
A program may use at most 128 MiB of HBM per device.

v0:
```python
import functools

import jax
import jax.numpy as jnp
from jax import lax
from jax.experimental import pallas as pl
from jax.experimental.pallas import tpu as pltpu
from jax.sharding import PartitionSpec as P

RATE = 4096.0
HALF = 0.5 * RATE
LANE = 128
MESH = pl.DeviceIdType.MESH


def peers(axis, me, count):
    return [{axis: lax.rem(me + step, count)} for step in range(1, count)]


def resolve(get, put, count):
    ratios = []
    values = []
    ratio = None
    value = None
    for k in range(count):
        diag = get(k, 0)
        rhs = get(k, 3)
        if k + 1 < count:
            diag = diag - get(k + 1, 1)
            rhs = rhs + get(k + 1, 4)
        if k > 0:
            link = get(k, 2)
            diag = diag - link * ratio
            rhs = rhs + link * value
        inv = 1.0 / diag
        value = rhs * inv
        values.append(value)
        if k + 1 < count:
            ratio = get(k + 1, 2) * inv
            ratios.append(ratio)
    for k in range(count - 2, -1, -1):
        values[k] = values[k] + ratios[k] * values[k + 1]
    for k in range(count):
        put(k, 1, values[k])
        put(k, 0, values[k - 1] if k > 0 else jnp.zeros_like(values[0]))


def kernel(
    dims,
    src_hbm,
    kap_hbm,
    mid_hbm,
    new_hbm,
    f,
    kap,
    kap_t,
    ft,
    rx,
    tx,
    ry,
    iy,
    ty,
    mid,
    new,
    halo_x,
    halo_y,
    sx,
    gx,
    bx,
    ox,
    sy,
    gy,
    by,
    oy,
    in_sem,
    out_sem,
    halo_send,
    halo_recv,
    x_send,
    x_recv,
    xb_send,
    xb_recv,
    y_send,
    y_recv,
    yb_send,
    yb_recv,
):
    nx, ny, rows, cols, tiles, per, chunks, share_x, share_y = dims
    ix = lax.axis_index("gx")
    iy_dev = lax.axis_index("gy")
    groups_x = cols // share_x
    groups_y = rows // share_y

    def lanes(l):
        return pl.ds(pl.multiple_of(l * LANE, LANE), LANE)

    kap_in = [
        pltpu.make_async_copy(kap_hbm.at[:, lanes(l)], kap.at[l], in_sem.at[0, l])
        for l in range(tiles)
    ]
    src_in = [
        pltpu.make_async_copy(src_hbm.at[:, lanes(l)], f.at[l], in_sem.at[1, l])
        for l in range(tiles)
    ]
    for copy in kap_in + src_in:
        copy.start()

    barrier = pltpu.get_barrier_semaphore()
    for target in peers("gx", ix, nx) + peers("gy", iy_dev, ny):
        pl.semaphore_signal(barrier, inc=1, device_id=target, device_id_type=MESH)
    pl.semaphore_wait(barrier, nx + ny - 2)

    def halo(slot, source, dest, target):
        return pltpu.make_async_remote_copy(
            src_ref=source,
            dst_ref=dest,
            send_sem=halo_send.at[slot],
            recv_sem=halo_recv.at[slot],
            device_id=target,
            device_id_type=MESH,
        )

    x_up = halo(0, kap_hbm.at[pl.ds((rows - 1) * cols, cols), :], halo_x.at[0], {"gx": lax.rem(ix + 1, nx)})
    x_down = halo(1, kap_hbm.at[pl.ds(0, cols), :], halo_x.at[1], {"gx": lax.rem(ix + nx - 1, nx)})
    y_up = halo(2, kap_t.at[:, pl.ds((cols - 1) * rows, rows), :], halo_y.at[0], {"gy": lax.rem(iy_dev + 1, ny)})
    y_down = halo(3, kap_t.at[:, pl.ds(0, rows), :], halo_y.at[1], {"gy": lax.rem(iy_dev + ny - 1, ny)})

    x_up.start()
    x_down.start()

    for l in range(tiles):
        kap_in[l].wait()

    def turn(l, carry):
        for i in range(rows):
            kap_t[l, pl.ds(i, cols, stride=rows), :] = kap[l, pl.ds(i * cols, cols), :]
        return carry

    lax.fori_loop(0, tiles, turn, 0)
    y_up.start()
    y_down.start()
    x_up.wait_recv()
    x_down.wait_recv()

    @pl.when(ix == 0)
    def _():
        halo_x[0] = jnp.zeros(halo_x.shape[1:], jnp.float32)

    @pl.when(ix == nx - 1)
    def _():
        halo_x[1] = jnp.zeros(halo_x.shape[1:], jnp.float32)

    def x_forward(l, chunk, part):
        def row(i):
            return kap[l, pl.ds(i * cols, cols), :]

        here = row(0)
        face = HALF * (halo_x[0, :, lanes(l)] + here)
        total = 1.0 + face
        link = face
        y = f[l, pl.ds(0, cols), :]
        p = None
        q = None
        for i in range(rows):
            at = pl.ds(i * cols, cols)
            if i > 0:
                total = 1.0 + ratio * total
                link = ratio * link
                y = f[l, at, :] + ratio * y
            after = row(i + 1) if i + 1 < rows else halo_x[1, :, lanes(l)]
            face = HALF * (here + after)
            here = after
            diag = total + face
            if i + 1 < rows:
                inv = 1.0 / diag
                ratio = face * inv
                t = link * inv
                p = t * link if p is None else p + t * link
                q = t * y if q is None else q + t * y
                rx[l, at, :] = ratio
                tx[l, at, :] = t
                f[l, at, :] = y * inv
        slots = pl.ds(part * groups_x, groups_x)
        for coef, value in enumerate((diag, p, link, y, q)):
            sx[chunk, slots, coef] = value.reshape(groups_x, share_x, LANE)

    def exchange(axis, me, count, chunk, source, dest, send_sem, recv_sem):
        return [
            pltpu.make_async_remote_copy(
                src_ref=source.at[chunk, lax.rem(me + step, count)],
                dst_ref=dest.at[chunk, me],
                send_sem=send_sem.at[chunk, step],
                recv_sem=recv_sem.at[chunk, step],
                device_id={axis: lax.rem(me + step, count)},
                device_id_type=MESH,
            )
            for step in range(1, count)
        ]

    def arrived(axis, me, count, chunk, source, dest, send_sem, recv_sem):
        for step in range(1, count):
            origin = lax.rem(me + count - step, count)
            pltpu.make_async_remote_copy(
                src_ref=source.at[chunk, origin],
                dst_ref=dest.at[chunk, origin],
                send_sem=send_sem.at[chunk, step],
                recv_sem=recv_sem.at[chunk, step],
                device_id={axis: origin},
                device_id_type=MESH,
            ).wait_recv()

    x_up_args = lambda c: ("gx", ix, nx, c, sx, gx, x_send, x_recv)
    x_back_args = lambda c: ("gx", ix, nx, c, bx, ox, xb_send, xb_recv)
    y_up_args = lambda c: ("gy", iy_dev, ny, c, sy, gy, y_send, y_recv)
    y_back_args = lambda c: ("gy", iy_dev, ny, c, by, oy, yb_send, yb_recv)
    pending = []

    def launch(args):
        copies = exchange(*args)
        for copy in copies:
            copy.start()
        pending.extend(copies)

    for c in range(chunks):
        for a in range(per):
            src_in[c * per + a].wait()

        def body(a, carry, c=c):
            x_forward(c * per + a, c, a)
            return carry

        lax.fori_loop(0, per, body, 0)
        launch(x_up_args(c))
        gx[c, ix] = sx[c, ix]

    y_up.wait_recv()
    y_down.wait_recv()

    @pl.when(iy_dev == 0)
    def _():
        halo_y[0] = jnp.zeros(halo_y.shape[1:], jnp.float32)

    @pl.when(iy_dev == ny - 1)
    def _():
        halo_y[1] = jnp.zeros(halo_y.shape[1:], jnp.float32)

    def y_factor(c):
        part = pl.ds(c * per, per)

        def row(j):
            return kap_t[part, pl.ds(j * rows, rows), :]

        here = row(0)
        face = HALF * (halo_y[0, part] + here)
        total = 1.0 + face
        link = face
        p = None
        for j in range(cols):
            at = pl.ds(j * rows, rows)
            if j > 0:
                total = 1.0 + ratio * total
                link = ratio * link
            after = row(j + 1) if j + 1 < cols else halo_y[1, part]
            face = HALF * (here + after)
            here = after
            diag = total + face
            if j + 1 < cols:
                inv = 1.0 / diag
                ratio = face * inv
                t = link * inv
                p = t * link if p is None else p + t * link
                ry[part, at, :] = ratio
                ty[part, at, :] = t
                iy[part, at, :] = inv
        for coef, value in enumerate((diag, p, link)):
            sy[c, :, coef] = value.reshape(per * groups_y, share_y, LANE)

    def factor_body(c, carry):
        y_factor(c)
        return carry

    lax.fori_loop(0, chunks, factor_body, 0)

    def solve_ends(chunk, got, back, count):
        def get(k, coef):
            return got[chunk, k, coef]

        def put(k, which, value):
            back[chunk, k, which] = value

        resolve(get, put, count)

    for c in range(chunks):
        arrived(*x_up_args(c))
        solve_ends(c, gx, bx, nx)
        launch(x_back_args(c))
        ox[c, ix] = bx[c, ix]

    def x_backward(l, chunk, part):
        slots = pl.ds(part * groups_x, groups_x)
        before = ox[chunk, slots, 0].reshape(cols, LANE)
        m = ox[chunk, slots, 1].reshape(cols, LANE)
        for i in range(rows - 1, -1, -1):
            at = pl.ds(i * cols, cols)
            if i + 1 < rows:
                m = f[l, at, :] + tx[l, at, :] * before + rx[l, at, :] * m
            mid[l, at, :] = m
            ft[l, pl.ds(i, cols, stride=rows), :] = m

    def y_forward(c):
        part = pl.ds(c * per, per)
        q = None
        for j in range(cols):
            at = pl.ds(j * rows, rows)
            y_now = ft[part, at, :]
            if j > 0:
                y_now = y_now + ry[part, pl.ds((j - 1) * rows, rows), :] * y
            y = y_now
            if j + 1 < cols:
                step = ty[part, at, :] * y
                q = step if q is None else q + step
                ft[part, at, :] = y * iy[part, at, :]
        for coef, value in ((3, y), (4, q)):
            sy[c, :, coef] = value.reshape(per * groups_y, share_y, LANE)

    outs = []
    for c in range(chunks):
        arrived(*x_back_args(c))

        def body(a, carry, c=c):
            x_backward(c * per + a, c, a)
            return carry

        lax.fori_loop(0, per, body, 0)
        y_forward(c)
        launch(y_up_args(c))
        gy[c, iy_dev] = sy[c, iy_dev]
        for a in range(per):
            l = c * per + a
            out = pltpu.make_async_copy(mid.at[l], mid_hbm.at[:, lanes(l)], out_sem.at[0, l])
            out.start()
            outs.append(out)

    for c in range(chunks):
        arrived(*y_up_args(c))
        solve_ends(c, gy, by, ny)
        launch(y_back_args(c))
        oy[c, iy_dev] = by[c, iy_dev]

    def y_backward(c):
        part = pl.ds(c * per, per)
        before = oy[c, :, 0].reshape(per, rows, LANE)
        n = oy[c, :, 1].reshape(per, rows, LANE)
        for j in range(cols - 1, -1, -1):
            at = pl.ds(j * rows, rows)
            if j + 1 < cols:
                n = ft[part, at, :] + ty[part, at, :] * before + ry[part, at, :] * n
            for a in range(per):
                new[c * per + a, pl.ds(j, rows, stride=cols), :] = n[a]

    for c in range(chunks):
        arrived(*y_back_args(c))
        y_backward(c)
        for a in range(per):
            l = c * per + a
            out = pltpu.make_async_copy(new.at[l], new_hbm.at[:, lanes(l)], out_sem.at[1, l])
            out.start()
            outs.append(out)

    for out in outs:
        out.wait()
    for copy in [x_up, x_down, y_up, y_down] + pending:
        copy.wait_send()


def per_device(source, conductivity):
    rows, cols, depth = source.shape
    nx = lax.axis_size("gx")
    ny = lax.axis_size("gy")
    tiles = depth // LANE
    per = min(tiles, max(1, 8 * nx // cols, 8 * ny // rows if ny * 8 <= rows * tiles else 1))
    chunks = tiles // per
    share_x = cols * per // nx
    share_y = rows * per // ny
    dims = (nx, ny, rows, cols, tiles, per, chunks, share_x, share_y)
    size = rows * cols
    f32 = jnp.float32
    block = pltpu.VMEM((tiles, size, LANE), f32)
    dma = pltpu.SemaphoreType.DMA
    flat = jax.ShapeDtypeStruct((size, depth), f32)
    mid, new = pl.pallas_call(
        functools.partial(kernel, dims),
        out_shape=(flat, flat),
        in_specs=[pl.BlockSpec(memory_space=pl.ANY)] * 2,
        out_specs=(pl.BlockSpec(memory_space=pl.ANY),) * 2,
        scratch_shapes=[block] * 11
        + [
            pltpu.VMEM((2, cols, depth), f32),
            pltpu.VMEM((2, tiles, rows, LANE), f32),
            pltpu.VMEM((chunks, nx, 5, share_x, LANE), f32),
            pltpu.VMEM((chunks, nx, 5, share_x, LANE), f32),
            pltpu.VMEM((chunks, nx, 2, share_x, LANE), f32),
            pltpu.VMEM((chunks, nx, 2, share_x, LANE), f32),
            pltpu.VMEM((chunks, ny, 5, share_y, LANE), f32),
            pltpu.VMEM((chunks, ny, 5, share_y, LANE), f32),
            pltpu.VMEM((chunks, ny, 2, share_y, LANE), f32),
            pltpu.VMEM((chunks, ny, 2, share_y, LANE), f32),
            dma((2, tiles)),
            dma((2, tiles)),
            dma((4,)),
            dma((4,)),
            dma((chunks, nx)),
            dma((chunks, nx)),
            dma((chunks, nx)),
            dma((chunks, nx)),
            dma((chunks, ny)),
            dma((chunks, ny)),
            dma((chunks, ny)),
            dma((chunks, ny)),
        ],
        compiler_params=pltpu.CompilerParams(
            collective_id=0, has_side_effects=True, vmem_limit_bytes=48 << 20
        ),
    )(source.reshape(size, depth), conductivity.reshape(size, depth))
    return mid.reshape(source.shape), new.reshape(source.shape)


def solution(mesh):
    return jax.shard_map(
        per_device,
        mesh=mesh,
        in_specs=(P("gx", "gy", None), P("gx", "gy", None)),
        out_specs=(P("gx", "gy", None), P("gx", "gy", None)),
        check_vma=False,
    )
```

profile of v0, /device:TPU:0, one launch (start us, length us, event | category | flops | bytes accessed | tf_op | source)
XLA Modules:
  0.0 36.8 jit_solution(6359691201107672124)
XLA Ops:
  0.6 0.0 copy-start
  0.6 1.2 %copy-done = f32[16,32,512]{2,1,0:T(8,128)S(1)} copy-done((f32[16,32,512]{2,1,0:T(8,128)S(1)}, f32[16,32,512]{2,1,0:T(8,128)}, u32[]{:S(2)}) %copy-start) | copy-done | bytes 1048600
  1.9 0.0 copy-start.1
  1.9 1.2 %copy-done.1 = f32[16,32,512]{2,1,0:T(8,128)S(1)} copy-done((f32[16,32,512]{2,1,0:T(8,128)S(1)}, f32[16,32,512]{2,1,0:T(8,128)}, u32[]{:S(2)}) %copy-start.1) | copy-done | bytes 1048600
  3.1 31.7 %shard_map.41 = (f32[512,512]{1,0:T(8,128)S(1)}, f32[512,512]{1,0:T(8,128)S(1)}) custom-call(f32[512,512]{1,0:T(8,128)S(1)} %bitcast.4, f32[512,512]{1,0:T(8,128)S(1)} %bitcast.5), custom_call_target="tpu_custom_call" | custom-call | tf_op jit(solution)/shard_map/pallas_call | solution.py:391
  34.8 1.0 %copy.6 = f32[16,32,512]{2,1,0:T(8,128)} copy(f32[16,32,512]{2,1,0:T(8,128)S(1)} %bitcast.7) | data formatting | bytes 2097152
  35.8 1.0 %copy.7 = f32[16,32,512]{2,1,0:T(8,128)} copy(f32[16,32,512]{2,1,0:T(8,128)S(1)} %bitcast.6) | data formatting | bytes 2097152
Async XLA Ops:
  0.6 1.2 %copy-start = (f32[16,32,512]{2,1,0:T(8,128)S(1)}, f32[16,32,512]{2,1,0:T(8,128)}, u32[]{:S(2)}) copy-start(f32[16,32,512]{2,1,0:T(8,128)} %param.2) | copy-start | bytes 3145732
  1.9 1.2 %copy-start.1 = (f32[16,32,512]{2,1,0:T(8,128)S(1)}, f32[16,32,512]{2,1,0:T(8,128)}, u32[]{:S(2)}) copy-start(f32[16,32,512]{2,1,0:T(8,128)} %param.3) | copy-start | bytes 3145732
where the time goes:
time: 37 us; the launch traced here: 36.8 us
  Pallas kernels  31.7 us (86%)
  local copies, waits for them, and re-layouts  4.38 us (12%)
  between operations  0.65 us (2%)
    pallas_call x1, Pallas kernels, per_device(): pl.pallas_call(functools.partial(kernel, dims), out_shape=(flat, flat), i...  31.7 us
    unnamed x6, local copies, waits for them, and re-layouts  4.38 us

commit v1 on v0

--- a/solution.py
+++ b/solution.py
@@ -49,37 +49,38 @@
     dims,
     src_hbm,
     kap_hbm,
-    mid_hbm,
-    new_hbm,
+    mid,
+    ft,
+    ry,
+    ty,
+    ends,
     f,
     kap,
     kap_t,
-    ft,
     rx,
     tx,
-    ry,
     iy,
-    ty,
-    mid,
-    new,
     halo_x,
     halo_y,
     sx,
     gx,
     bx,
     ox,
+    sa,
+    ga,
     sy,
     gy,
     by,
     oy,
     in_sem,
-    out_sem,
     halo_send,
     halo_recv,
     x_send,
     x_recv,
     xb_send,
     xb_recv,
+    a_send,
+    a_recv,
     y_send,
     y_recv,
     yb_send,
@@ -125,8 +126,10 @@
     y_up = halo(2, kap_t.at[:, pl.ds((cols - 1) * rows, rows), :], halo_y.at[0], {"gy": lax.rem(iy_dev + 1, ny)})
     y_down = halo(3, kap_t.at[:, pl.ds(0, rows), :], halo_y.at[1], {"gy": lax.rem(iy_dev + ny - 1, ny)})
 
-    x_up.start()
-    x_down.start()
+    x_more, x_less = ix < nx - 1, ix > 0
+    y_more, y_less = iy_dev < ny - 1, iy_dev > 0
+    pl.when(x_more)(x_up.start)
+    pl.when(x_less)(x_down.start)
 
     for l in range(tiles):
         kap_in[l].wait()
@@ -137,10 +140,10 @@
         return carry
 
     lax.fori_loop(0, tiles, turn, 0)
-    y_up.start()
-    y_down.start()
-    x_up.wait_recv()
-    x_down.wait_recv()
+    pl.when(y_more)(y_up.start)
+    pl.when(y_less)(y_down.start)
+    pl.when(x_less)(x_up.wait_recv)
+    pl.when(x_more)(x_down.wait_recv)
 
     @pl.when(ix == 0)
     def _():
@@ -212,6 +215,7 @@
     x_up_args = lambda c: ("gx", ix, nx, c, sx, gx, x_send, x_recv)
     x_back_args = lambda c: ("gx", ix, nx, c, bx, ox, xb_send, xb_recv)
     y_up_args = lambda c: ("gy", iy_dev, ny, c, sy, gy, y_send, y_recv)
+    a_args = ("gy", iy_dev, ny, 0, sa, ga, a_send, a_recv)
     y_back_args = lambda c: ("gy", iy_dev, ny, c, by, oy, yb_send, yb_recv)
     pending = []
 
@@ -233,8 +237,8 @@
         launch(x_up_args(c))
         gx[c, ix] = sx[c, ix]
 
-    y_up.wait_recv()
-    y_down.wait_recv()
+    pl.when(y_less)(y_up.wait_recv)
+    pl.when(y_more)(y_down.wait_recv)
 
     @pl.when(iy_dev == 0)
     def _():
@@ -273,26 +277,37 @@
                 ty[part, at, :] = t
                 iy[part, at, :] = inv
         for coef, value in enumerate((diag, p, link)):
-            sy[c, :, coef] = value.reshape(per * groups_y, share_y, LANE)
+            sa[0, :, c, coef] = value.reshape(per * groups_y, share_y, LANE)
 
     def factor_body(c, carry):
         y_factor(c)
         return carry
 
     lax.fori_loop(0, chunks, factor_body, 0)
-
-    def solve_ends(chunk, got, back, count):
+    launch(a_args)
+    ga[0, iy_dev] = sa[0, iy_dev]
+
+    def solve_x(c):
         def get(k, coef):
-            return got[chunk, k, coef]
+            return gx[c, k, coef]
 
         def put(k, which, value):
-            back[chunk, k, which] = value
-
-        resolve(get, put, count)
+            bx[c, k, which] = value
+
+        resolve(get, put, nx)
+
+    def solve_y(c):
+        def get(k, coef):
+            return ga[0, k, c, coef] if coef < 3 else gy[c, k, coef - 3]
+
+        def put(k, which, value):
+            by[c, k, which] = value
+
+        resolve(get, put, ny)
 
     for c in range(chunks):
         arrived(*x_up_args(c))
-        solve_ends(c, gx, bx, nx)
+        solve_x(c)
         launch(x_back_args(c))
         ox[c, ix] = bx[c, ix]
 
@@ -320,10 +335,9 @@
                 step = ty[part, at, :] * y
                 q = step if q is None else q + step
                 ft[part, at, :] = y * iy[part, at, :]
-        for coef, value in ((3, y), (4, q)):
+        for coef, value in enumerate((y, q)):
             sy[c, :, coef] = value.reshape(per * groups_y, share_y, LANE)
 
-    outs = []
     for c in range(chunks):
         arrived(*x_back_args(c))
 
@@ -335,42 +349,53 @@
         y_forward(c)
         launch(y_up_args(c))
         gy[c, iy_dev] = sy[c, iy_dev]
-        for a in range(per):
-            l = c * per + a
-            out = pltpu.make_async_copy(mid.at[l], mid_hbm.at[:, lanes(l)], out_sem.at[0, l])
-            out.start()
-            outs.append(out)
-
+
+    arrived(*a_args)
     for c in range(chunks):
         arrived(*y_up_args(c))
-        solve_ends(c, gy, by, ny)
+        solve_y(c)
         launch(y_back_args(c))
         oy[c, iy_dev] = by[c, iy_dev]
 
-    def y_backward(c):
+    for c in range(chunks):
+        arrived(*y_back_args(c))
+        ends[c] = oy[c]
+
+    for copy in pending:
+        copy.wait_send()
+    pl.when(x_more)(x_up.wait_send)
+    pl.when(x_less)(x_down.wait_send)
+    pl.when(y_more)(y_up.wait_send)
+    pl.when(y_less)(y_down.wait_send)
+
+
+def finish(dims, mid, ft, ry, ty, ends, mid_hbm, new_hbm, new, out_sem):
+    nx, ny, rows, cols, tiles, per, chunks, share_x, share_y = dims
+    outs = []
+
+    def send(source, dest, which, l):
+        out = pltpu.make_async_copy(
+            source.at[l], dest.at[:, pl.ds(l * LANE, LANE)], out_sem.at[which, l]
+        )
+        out.start()
+        outs.append(out)
+
+    for l in range(tiles):
+        send(mid, mid_hbm, 0, l)
+    for c in range(chunks):
         part = pl.ds(c * per, per)
-        before = oy[c, :, 0].reshape(per, rows, LANE)
-        n = oy[c, :, 1].reshape(per, rows, LANE)
+        before = ends[c, :, 0].reshape(per, rows, LANE)
+        n = ends[c, :, 1].reshape(per, rows, LANE)
         for j in range(cols - 1, -1, -1):
             at = pl.ds(j * rows, rows)
             if j + 1 < cols:
                 n = ft[part, at, :] + ty[part, at, :] * before + ry[part, at, :] * n
             for a in range(per):
                 new[c * per + a, pl.ds(j, rows, stride=cols), :] = n[a]
-
-    for c in range(chunks):
-        arrived(*y_back_args(c))
-        y_backward(c)
         for a in range(per):
-            l = c * per + a
-            out = pltpu.make_async_copy(new.at[l], new_hbm.at[:, lanes(l)], out_sem.at[1, l])
-            out.start()
-            outs.append(out)
-
+            send(new, new_hbm, 1, c * per + a)
     for out in outs:
         out.wait()
-    for copy in [x_up, x_down, y_up, y_down] + pending:
-        copy.wait_send()
 
 
 def per_device(source, conductivity):
@@ -386,14 +411,17 @@
     size = rows * cols
     f32 = jnp.float32
     block = pltpu.VMEM((tiles, size, LANE), f32)
+    ends = pltpu.VMEM((chunks, ny, 2, share_y, LANE), f32)
     dma = pltpu.SemaphoreType.DMA
     flat = jax.ShapeDtypeStruct((size, depth), f32)
-    mid, new = pl.pallas_call(
+    hbm = pl.BlockSpec(memory_space=pltpu.HBM)
+    vmem = pl.BlockSpec(memory_space=pltpu.VMEM)
+    parts = pl.pallas_call(
         functools.partial(kernel, dims),
-        out_shape=(flat, flat),
-        in_specs=[pl.BlockSpec(memory_space=pl.ANY)] * 2,
-        out_specs=(pl.BlockSpec(memory_space=pl.ANY),) * 2,
-        scratch_shapes=[block] * 11
+        out_shape=(block,) * 4 + (ends,),
+        in_specs=[hbm] * 2,
+        out_specs=(vmem,) * 5,
+        scratch_shapes=[block] * 6
         + [
             pltpu.VMEM((2, cols, depth), f32),
             pltpu.VMEM((2, tiles, rows, LANE), f32),
@@ -401,11 +429,12 @@
             pltpu.VMEM((chunks, nx, 5, share_x, LANE), f32),
             pltpu.VMEM((chunks, nx, 2, share_x, LANE), f32),
             pltpu.VMEM((chunks, nx, 2, share_x, LANE), f32),
-            pltpu.VMEM((chunks, ny, 5, share_y, LANE), f32),
-            pltpu.VMEM((chunks, ny, 5, share_y, LANE), f32),
+            pltpu.VMEM((1, ny, chunks, 3, share_y, LANE), f32),
+            pltpu.VMEM((1, ny, chunks, 3, share_y, LANE), f32),
             pltpu.VMEM((chunks, ny, 2, share_y, LANE), f32),
             pltpu.VMEM((chunks, ny, 2, share_y, LANE), f32),
-            dma((2, tiles)),
+            ends,
+            ends,
             dma((2, tiles)),
             dma((4,)),
             dma((4,)),
@@ -413,15 +442,25 @@
             dma((chunks, nx)),
             dma((chunks, nx)),
             dma((chunks, nx)),
+            dma((1, ny)),
+            dma((1, ny)),
             dma((chunks, ny)),
             dma((chunks, ny)),
             dma((chunks, ny)),
             dma((chunks, ny)),
         ],
         compiler_params=pltpu.CompilerParams(
-            collective_id=0, has_side_effects=True, vmem_limit_bytes=48 << 20
+            collective_id=0, has_side_effects=True, vmem_limit_bytes=32 << 20
         ),
-    )(source.reshape(size, depth), conductivity.reshape(size, depth))
+    )(*(pltpu.with_memory_space_constraint(x.reshape(size, depth), pltpu.HBM) for x in (source, conductivity)))
+    mid, new = pl.pallas_call(
+        functools.partial(finish, dims),
+        out_shape=(flat, flat),
+        in_specs=[vmem] * 5,
+        out_specs=(hbm, hbm),
+        scratch_shapes=[block, dma((2, tiles))],
+        compiler_params=pltpu.CompilerParams(vmem_limit_bytes=32 << 20),
+    )(*parts)
     return mid.reshape(source.shape), new.reshape(source.shape)
 
 

time: 37 us -> 32.3 us (0.87)
  local copies, waits for them, and re-layouts: 4.38 us -> 0 us
    unnamed x6 -> x0, local copies, waits for them, and re-layouts: 4.38 us -> none
    pallas_call x1 -> x2, Pallas kernels: 31.7 us -> 31.5 us  [the longest x1 29.6 us: per_device(): pl.pallas_call(functools.partial(kernel, dims), out_shape=(block,) * 4 +...]
where the time goes in v1:
time: 32.3 us; the launch traced here: 32.2 us
  Pallas kernels  31.5 us (98%)
  between operations  0.64 us (2%)
    pallas_call x1, Pallas kernels, per_device(): pl.pallas_call(functools.partial(kernel, dims), out_shape=(block,) * 4 +...  29.6 us
    pallas_call x1, Pallas kernels, per_device(): pl.pallas_call(functools.partial(finish, dims), out_shape=(flat, flat), i...  1.91 us

profile of v1, /device:TPU:0, one launch (start us, length us, event | category | flops | bytes accessed | tf_op | source)
XLA Modules:
  0.0 32.2 jit_solution(9781793023202644654)
XLA Ops:
  0.6 29.6 %shard_map.41 = (f32[4,512,128]{2,1,0:T(8,128)S(1)}, f32[4,512,128]{2,1,0:T(8,128)S(1)}, f32[4,512,128]{2,1,0:T(8,128)S(1)}, f32[4,512,128]{2,1,0:T(8,128)S(1)}, f32[2,4,2,8,128]{4,3,2,1,0:T(8,128)S(1)}) custom-call(f32[512,512]{1,0:T(8,128)} %bitcast.4, f32[512,512]{1,0:T(8,128)} %bitcast.5), custom_call_target="tpu_custom_call" | custom-call | tf_op jit(solution)/shard_map/pallas_call | solution.py:419
  30.3 1.9 %shard_map.42 = (f32[512,512]{1,0:T(8,128)}, f32[512,512]{1,0:T(8,128)}) custom-call(f32[4,512,128]{2,1,0:T(8,128)S(1)} %get-tuple-element.9.mid, f32[4,512,128]{2,1,0:T(8,128)S(1)} %get-tuple-element.10.ft, f32[4,512,128]{2,1,0:T(8,128)S(1)} %get-tuple-element.11.ry, f32[4,512,128]{2,1,0:T(8,128)S(1)} %get-tuple-element.12.ty, ...), custom_call_target="tpu_custom_call" | custom-call | tf_op jit(solution)/shard_map/pallas_call | solution.py:456

commit v2 on v1

--- a/solution.py
+++ b/solution.py
@@ -63,8 +63,12 @@
     halo_x,
     halo_y,
     sx,
-    gx,
-    bx,
+    ab,
+    zx,
+    gz,
+    bz,
+    oz,
+    tri,
     ox,
     sa,
     ga,
@@ -75,10 +79,14 @@
     in_sem,
     halo_send,
     halo_recv,
-    x_send,
-    x_recv,
-    xb_send,
-    xb_recv,
+    pair_send,
+    pair_recv,
+    z_send,
+    z_recv,
+    zb_send,
+    zb_recv,
+    pb_send,
+    pb_recv,
     a_send,
     a_recv,
     y_send,
@@ -89,6 +97,10 @@
     nx, ny, rows, cols, tiles, per, chunks, share_x, share_y = dims
     ix = lax.axis_index("gx")
     iy_dev = lax.axis_index("gy")
+    nz = nx // 2
+    core = lax.rem(ix, 2)
+    iz = lax.div(ix, 2)
+    partner = {"gx": ix + 1 - 2 * core}
     groups_x = cols // share_x
     groups_y = rows // share_y
 
@@ -187,6 +199,9 @@
         for coef, value in enumerate((diag, p, link, y, q)):
             sx[chunk, slots, coef] = value.reshape(groups_x, share_x, LANE)
 
+    def place(axis, index):
+        return {"gx": 2 * index + core} if axis == "z" else {axis: index}
+
     def exchange(axis, me, count, chunk, source, dest, send_sem, recv_sem):
         return [
             pltpu.make_async_remote_copy(
@@ -194,7 +209,7 @@
                 dst_ref=dest.at[chunk, me],
                 send_sem=send_sem.at[chunk, step],
                 recv_sem=recv_sem.at[chunk, step],
-                device_id={axis: lax.rem(me + step, count)},
+                device_id=place(axis, lax.rem(me + step, count)),
                 device_id_type=MESH,
             )
             for step in range(1, count)
@@ -208,12 +223,49 @@
                 dst_ref=dest.at[chunk, origin],
                 send_sem=send_sem.at[chunk, step],
                 recv_sem=recv_sem.at[chunk, step],
-                device_id={axis: origin},
+                device_id=place(axis, origin),
                 device_id_type=MESH,
             ).wait_recv()
 
-    x_up_args = lambda c: ("gx", ix, nx, c, sx, gx, x_send, x_recv)
-    x_back_args = lambda c: ("gx", ix, nx, c, bx, ox, xb_send, xb_recv)
+    x_up_args = lambda c: ("z", iz, nz, c, zx, gz, z_send, z_recv)
+    x_back_args = lambda c: ("z", iz, nz, c, bz, oz, zb_send, zb_recv)
+    own_half = pl.ds(core * nz, nz)
+    other_half = pl.ds((1 - core) * nz, nz)
+
+    def pair_up(c):
+        return pltpu.make_async_remote_copy(
+            src_ref=sx.at[c, other_half],
+            dst_ref=ab.at[c, core],
+            send_sem=pair_send.at[c],
+            recv_sem=pair_recv.at[c],
+            device_id=partner,
+            device_id_type=MESH,
+        )
+
+    def pair_back(c):
+        return pltpu.make_async_remote_copy(
+            src_ref=tri.at[c, pl.ds(1 - core, 2)],
+            dst_ref=ox.at[c, :, own_half],
+            send_sem=pb_send.at[c],
+            recv_sem=pb_recv.at[c],
+            device_id=partner,
+            device_id_type=MESH,
+        )
+
+    def merge(c):
+        diag = ab[c, 0, :, 0] - ab[c, 1, :, 1]
+        inv = 1.0 / diag
+        low = ab[c, 0, :, 2]
+        high = ab[c, 1, :, 2]
+        base = (ab[c, 0, :, 3] + ab[c, 1, :, 4]) * inv
+        to_low = low * inv
+        to_high = high * inv
+        zx[c, :, 0] = ab[c, 1, :, 0] - high * to_high
+        zx[c, :, 1] = ab[c, 0, :, 1] + low * to_low
+        zx[c, :, 2] = low * to_high
+        zx[c, :, 3] = ab[c, 1, :, 3] + high * base
+        zx[c, :, 4] = ab[c, 0, :, 4] + low * base
+        return base, to_low, to_high
     y_up_args = lambda c: ("gy", iy_dev, ny, c, sy, gy, y_send, y_recv)
     a_args = ("gy", iy_dev, ny, 0, sa, ga, a_send, a_recv)
     y_back_args = lambda c: ("gy", iy_dev, ny, c, by, oy, yb_send, yb_recv)
@@ -234,8 +286,17 @@
             return carry
 
         lax.fori_loop(0, per, body, 0)
+        copy = pair_up(c)
+        copy.start()
+        pending.append(copy)
+        ab[c, core] = sx[c, own_half]
+
+    merged = []
+    for c in range(chunks):
+        pair_up(c).wait_recv()
+        merged.append(merge(c))
         launch(x_up_args(c))
-        gx[c, ix] = sx[c, ix]
+        gz[c, iz] = zx[c, iz]
 
     pl.when(y_less)(y_up.wait_recv)
     pl.when(y_more)(y_down.wait_recv)
@@ -289,12 +350,12 @@
 
     def solve_x(c):
         def get(k, coef):
-            return gx[c, k, coef]
+            return gz[c, k, coef]
 
         def put(k, which, value):
-            bx[c, k, which] = value
-
-        resolve(get, put, nx)
+            bz[c, k, which] = value
+
+        resolve(get, put, nz)
 
     def solve_y(c):
         def get(k, coef):
@@ -309,12 +370,12 @@
         arrived(*x_up_args(c))
         solve_x(c)
         launch(x_back_args(c))
-        ox[c, ix] = bx[c, ix]
+        oz[c, iz] = bz[c, iz]
 
     def x_backward(l, chunk, part):
         slots = pl.ds(part * groups_x, groups_x)
-        before = ox[chunk, slots, 0].reshape(cols, LANE)
-        m = ox[chunk, slots, 1].reshape(cols, LANE)
+        before = ox[chunk, 0, slots].reshape(cols, LANE)
+        m = ox[chunk, 1, slots].reshape(cols, LANE)
         for i in range(rows - 1, -1, -1):
             at = pl.ds(i * cols, cols)
             if i + 1 < rows:
@@ -340,6 +401,19 @@
 
     for c in range(chunks):
         arrived(*x_back_args(c))
+        base, to_low, to_high = merged[c]
+        before = oz[c, :, 0]
+        last = oz[c, :, 1]
+        tri[c, 0] = before
+        tri[c, 1] = base + to_low * before + to_high * last
+        tri[c, 2] = last
+        copy = pair_back(c)
+        copy.start()
+        pending.append(copy)
+        ox[c, :, own_half] = tri[c, pl.ds(core, 2)]
+
+    for c in range(chunks):
+        pair_back(c).wait_recv()
 
         def body(a, carry, c=c):
             x_backward(c * per + a, c, a)
@@ -409,6 +483,7 @@
     share_y = rows * per // ny
     dims = (nx, ny, rows, cols, tiles, per, chunks, share_x, share_y)
     size = rows * cols
+    nz = nx // 2
     f32 = jnp.float32
     block = pltpu.VMEM((tiles, size, LANE), f32)
     ends = pltpu.VMEM((chunks, ny, 2, share_y, LANE), f32)
@@ -426,9 +501,13 @@
             pltpu.VMEM((2, cols, depth), f32),
             pltpu.VMEM((2, tiles, rows, LANE), f32),
             pltpu.VMEM((chunks, nx, 5, share_x, LANE), f32),
-            pltpu.VMEM((chunks, nx, 5, share_x, LANE), f32),
-            pltpu.VMEM((chunks, nx, 2, share_x, LANE), f32),
-            pltpu.VMEM((chunks, nx, 2, share_x, LANE), f32),
+            pltpu.VMEM((chunks, 2, nz, 5, share_x, LANE), f32),
+            pltpu.VMEM((chunks, nz, 5, share_x, LANE), f32),
+            pltpu.VMEM((chunks, nz, 5, share_x, LANE), f32),
+            pltpu.VMEM((chunks, nz, 2, share_x, LANE), f32),
+            pltpu.VMEM((chunks, nz, 2, share_x, LANE), f32),
+            pltpu.VMEM((chunks, 3, nz, share_x, LANE), f32),
+            pltpu.VMEM((chunks, 2, nx, share_x, LANE), f32),
             pltpu.VMEM((1, ny, chunks, 3, share_y, LANE), f32),
             pltpu.VMEM((1, ny, chunks, 3, share_y, LANE), f32),
             pltpu.VMEM((chunks, ny, 2, share_y, LANE), f32),
@@ -438,10 +517,14 @@
             dma((2, tiles)),
             dma((4,)),
             dma((4,)),
-            dma((chunks, nx)),
-            dma((chunks, nx)),
-            dma((chunks, nx)),
-            dma((chunks, nx)),
+            dma((chunks,)),
+            dma((chunks,)),
+            dma((chunks, nz)),
+            dma((chunks, nz)),
+            dma((chunks, nz)),
+            dma((chunks, nz)),
+            dma((chunks,)),
+            dma((chunks,)),
             dma((1, ny)),
             dma((1, ny)),
             dma((chunks, ny)),

time: 32.3 us -> 29.9 us (0.926)
  Pallas kernels: 31.5 us -> 29.1 us
    pallas_call x1, Pallas kernels: 29.6 us -> 27.2 us  [per_device(): pl.pallas_call(functools.partial(kernel, dims), out_shape=(block,) * 4 +...]
where the time goes in v2:
time: 29.9 us; the launch traced here: 29.8 us
  Pallas kernels  29.1 us (97%)
  between operations  0.64 us (2%)
    pallas_call x1, Pallas kernels, per_device(): pl.pallas_call(functools.partial(kernel, dims), out_shape=(block,) * 4 +...  27.2 us
    pallas_call x1, Pallas kernels, per_device(): pl.pallas_call(functools.partial(finish, dims), out_shape=(flat, flat), i...  1.91 us

profile of v2, /device:TPU:0, one launch (start us, length us, event | category | flops | bytes accessed | tf_op | source)
XLA Modules:
  0.0 29.8 jit_solution(14419680842458966779)
XLA Ops:
  0.6 27.2 %shard_map.41 = (f32[4,512,128]{2,1,0:T(8,128)S(1)}, f32[4,512,128]{2,1,0:T(8,128)S(1)}, f32[4,512,128]{2,1,0:T(8,128)S(1)}, f32[4,512,128]{2,1,0:T(8,128)S(1)}, f32[2,4,2,8,128]{4,3,2,1,0:T(8,128)S(1)}) custom-call(f32[512,512]{1,0:T(8,128)} %bitcast.4, f32[512,512]{1,0:T(8,128)} %bitcast.5), custom_call_target="tpu_custom_call" | custom-call | tf_op jit(solution)/shard_map/pallas_call | solution.py:494
  27.9 1.9 %shard_map.42 = (f32[512,512]{1,0:T(8,128)}, f32[512,512]{1,0:T(8,128)}) custom-call(f32[4,512,128]{2,1,0:T(8,128)S(1)} %get-tuple-element.9.mid, f32[4,512,128]{2,1,0:T(8,128)S(1)} %get-tuple-element.10.ft, f32[4,512,128]{2,1,0:T(8,128)S(1)} %get-tuple-element.11.ry, f32[4,512,128]{2,1,0:T(8,128)S(1)} %get-tuple-element.12.ty, ...), custom_call_target="tpu_custom_call" | custom-call | tf_op jit(solution)/shard_map/pallas_call | solution.py:539

commit v3 on v2

--- a/solution.py
+++ b/solution.py
@@ -133,15 +133,12 @@
             device_id_type=MESH,
         )
 
-    x_up = halo(0, kap_hbm.at[pl.ds((rows - 1) * cols, cols), :], halo_x.at[0], {"gx": lax.rem(ix + 1, nx)})
-    x_down = halo(1, kap_hbm.at[pl.ds(0, cols), :], halo_x.at[1], {"gx": lax.rem(ix + nx - 1, nx)})
+    x_edge = halo(0, kap_hbm.at[pl.ds((1 - core) * ((rows - 1) * cols), cols), :], halo_x, partner)
     y_up = halo(2, kap_t.at[:, pl.ds((cols - 1) * rows, rows), :], halo_y.at[0], {"gy": lax.rem(iy_dev + 1, ny)})
     y_down = halo(3, kap_t.at[:, pl.ds(0, rows), :], halo_y.at[1], {"gy": lax.rem(iy_dev + ny - 1, ny)})
 
-    x_more, x_less = ix < nx - 1, ix > 0
     y_more, y_less = iy_dev < ny - 1, iy_dev > 0
-    pl.when(x_more)(x_up.start)
-    pl.when(x_less)(x_down.start)
+    x_edge.start()
 
     for l in range(tiles):
         kap_in[l].wait()
@@ -154,49 +151,57 @@
     lax.fori_loop(0, tiles, turn, 0)
     pl.when(y_more)(y_up.start)
     pl.when(y_less)(y_down.start)
-    pl.when(x_less)(x_up.wait_recv)
-    pl.when(x_more)(x_down.wait_recv)
-
-    @pl.when(ix == 0)
-    def _():
-        halo_x[0] = jnp.zeros(halo_x.shape[1:], jnp.float32)
-
-    @pl.when(ix == nx - 1)
-    def _():
-        halo_x[1] = jnp.zeros(halo_x.shape[1:], jnp.float32)
+    x_edge.wait_recv()
+    lower = core == 0
 
     def x_forward(l, chunk, part):
         def row(i):
             return kap[l, pl.ds(i * cols, cols), :]
 
         here = row(0)
-        face = HALF * (halo_x[0, :, lanes(l)] + here)
+        first = here
+        source = f[l, pl.ds(0, cols), :]
+        face = HALF * (halo_x[:, lanes(l)] + here)
         total = 1.0 + face
         link = face
-        y = f[l, pl.ds(0, cols), :]
-        p = None
-        q = None
+        y = source
         for i in range(rows):
             at = pl.ds(i * cols, cols)
-            if i > 0:
+            if i == 1:
+                total = 1.0 + jnp.where(lower, face, ratio * total)
+                link = jnp.where(lower, face, ratio * link)
+                y = f[l, at, :] + jnp.where(lower, 0.0, ratio * y)
+            elif i > 1:
                 total = 1.0 + ratio * total
                 link = ratio * link
                 y = f[l, at, :] + ratio * y
-            after = row(i + 1) if i + 1 < rows else halo_x[1, :, lanes(l)]
+            after = row(i + 1) if i + 1 < rows else halo_x[:, lanes(l)]
             face = HALF * (here + after)
+            if i + 1 == rows:
+                face = jnp.where(lower, face, 0.0)
+                edge = jnp.where(lower, first, here)
             here = after
             diag = total + face
-            if i + 1 < rows:
+            if i == 0:
                 inv = 1.0 / diag
                 ratio = face * inv
                 t = link * inv
-                p = t * link if p is None else p + t * link
-                q = t * y if q is None else q + t * y
+                p = jnp.where(lower, -1.0 - face, t * link)
+                q = jnp.where(lower, source, t * y)
+                rx[l, at, :] = jnp.where(lower, 0.0, ratio)
+                tx[l, at, :] = jnp.where(lower, 1.0, t)
+                f[l, at, :] = jnp.where(lower, 0.0, y * inv)
+            elif i + 1 < rows:
+                inv = 1.0 / diag
+                ratio = face * inv
+                t = link * inv
+                p = p + t * link
+                q = q + t * y
                 rx[l, at, :] = ratio
                 tx[l, at, :] = t
                 f[l, at, :] = y * inv
         slots = pl.ds(part * groups_x, groups_x)
-        for coef, value in enumerate((diag, p, link, y, q)):
+        for coef, value in enumerate((diag, p, link, y, q, edge)):
             sx[chunk, slots, coef] = value.reshape(groups_x, share_x, LANE)
 
     def place(axis, index):
@@ -265,6 +270,8 @@
         zx[c, :, 2] = low * to_high
         zx[c, :, 3] = ab[c, 1, :, 3] + high * base
         zx[c, :, 4] = ab[c, 0, :, 4] + low * base
+        zx[c, :, 5] = ab[c, 0, :, 5]
+        zx[c, :, 6] = ab[c, 1, :, 5]
         return base, to_low, to_high
     y_up_args = lambda c: ("gy", iy_dev, ny, c, sy, gy, y_send, y_recv)
     a_args = ("gy", iy_dev, ny, 0, sa, ga, a_send, a_recv)
@@ -349,13 +356,37 @@
     ga[0, iy_dev] = sa[0, iy_dev]
 
     def solve_x(c):
-        def get(k, coef):
-            return gz[c, k, coef]
+        below = [HALF * gz[c, k, 5] for k in range(nz)]
+        above = [HALF * gz[c, k, 6] for k in range(nz)]
+        face = [below[k] + above[k - 1] if k > 0 else below[0] for k in range(nz)] + [above[-1]]
+        parts = []
+        firsts = []
+        for k in range(nz):
+            inv = 1.0 / (face[k] - gz[c, k, 1])
+            link = gz[c, k, 2]
+            drive = gz[c, k, 4] * inv
+            to_low = face[k] * inv
+            to_high = link * inv
+            firsts.append((drive, to_low, to_high))
+            parts.append(
+                (
+                    gz[c, k, 0] + face[k + 1] - link * to_high,
+                    face[k] * to_low,
+                    link * to_low,
+                    gz[c, k, 3] + link * drive,
+                    face[k] * drive,
+                )
+            )
+        ends = {}
 
         def put(k, which, value):
-            bz[c, k, which] = value
-
-        resolve(get, put, nz)
+            ends[k, which] = value
+
+        resolve(lambda k, coef: parts[k][coef], put, nz)
+        for k in range(nz):
+            drive, to_low, to_high = firsts[k]
+            bz[c, k, 0] = drive + to_low * ends[k, 0] + to_high * ends[k, 1]
+            bz[c, k, 1] = ends[k, 1]
 
     def solve_y(c):
         def get(k, coef):
@@ -437,8 +468,7 @@
 
     for copy in pending:
         copy.wait_send()
-    pl.when(x_more)(x_up.wait_send)
-    pl.when(x_less)(x_down.wait_send)
+    x_edge.wait_send()
     pl.when(y_more)(y_up.wait_send)
     pl.when(y_less)(y_down.wait_send)
 
@@ -498,12 +528,12 @@
         out_specs=(vmem,) * 5,
         scratch_shapes=[block] * 6
         + [
-            pltpu.VMEM((2, cols, depth), f32),
+            pltpu.VMEM((cols, depth), f32),
             pltpu.VMEM((2, tiles, rows, LANE), f32),
-            pltpu.VMEM((chunks, nx, 5, share_x, LANE), f32),
-            pltpu.VMEM((chunks, 2, nz, 5, share_x, LANE), f32),
-            pltpu.VMEM((chunks, nz, 5, share_x, LANE), f32),
-            pltpu.VMEM((chunks, nz, 5, share_x, LANE), f32),
+            pltpu.VMEM((chunks, nx, 6, share_x, LANE), f32),
+            pltpu.VMEM((chunks, 2, nz, 6, share_x, LANE), f32),
+            pltpu.VMEM((chunks, nz, 7, share_x, LANE), f32),
+            pltpu.VMEM((chunks, nz, 7, share_x, LANE), f32),
             pltpu.VMEM((chunks, nz, 2, share_x, LANE), f32),
             pltpu.VMEM((chunks, nz, 2, share_x, LANE), f32),
             pltpu.VMEM((chunks, 3, nz, share_x, LANE), f32),

time: 29.9 us -> 29.6 us (0.990)
  Pallas kernels: 29.1 us -> 28.8 us
    pallas_call x1, Pallas kernels: 27.2 us -> 26.9 us  [per_device(): pl.pallas_call(functools.partial(kernel, dims), out_shape=(block,) * 4 +...]
where the time goes in v3:
time: 29.6 us; the launch traced here: 29.5 us
  Pallas kernels  28.8 us (97%)
  between operations  0.64 us (2%)
    pallas_call x1, Pallas kernels, per_device(): pl.pallas_call(functools.partial(kernel, dims), out_shape=(block,) * 4 +...  26.9 us
    pallas_call x1, Pallas kernels, per_device(): pl.pallas_call(functools.partial(finish, dims), out_shape=(flat, flat), i...  1.91 us

profile of v3, /device:TPU:0, one launch (start us, length us, event | category | flops | bytes accessed | tf_op | source)
XLA Modules:
  0.0 29.5 jit_solution(1342344728202357435)
XLA Ops:
  0.6 26.9 %shard_map.41 = (f32[4,512,128]{2,1,0:T(8,128)S(1)}, f32[4,512,128]{2,1,0:T(8,128)S(1)}, f32[4,512,128]{2,1,0:T(8,128)S(1)}, f32[4,512,128]{2,1,0:T(8,128)S(1)}, f32[2,4,2,8,128]{4,3,2,1,0:T(8,128)S(1)}) custom-call(f32[512,512]{1,0:T(8,128)} %bitcast.4, f32[512,512]{1,0:T(8,128)} %bitcast.5), custom_call_target="tpu_custom_call" | custom-call | tf_op jit(solution)/shard_map/pallas_call | solution.py:524
  27.6 1.9 %shard_map.42 = (f32[512,512]{1,0:T(8,128)}, f32[512,512]{1,0:T(8,128)}) custom-call(f32[4,512,128]{2,1,0:T(8,128)S(1)} %get-tuple-element.9.mid, f32[4,512,128]{2,1,0:T(8,128)S(1)} %get-tuple-element.10.ft, f32[4,512,128]{2,1,0:T(8,128)S(1)} %get-tuple-element.11.ry, f32[4,512,128]{2,1,0:T(8,128)S(1)} %get-tuple-element.12.ty, ...), custom_call_target="tpu_custom_call" | custom-call | tf_op jit(solution)/shard_map/pallas_call | solution.py:569
